TPU v7x, 32 devices: a whole 2x2x4 slice. The times are simulated.
32 devices in a mesh: groups: 2 (over x), rows: 16 (over z, y, core).
Axes of the slice: x: 2, y: 2, z: 4, core: 2. Of those that a mesh axis runs over, the one named last changes fastest.
Arguments:
- bin_ids: int32 [16384, 512], P(('groups', 'rows')), parts along dimension 0, may hold values from 0 to 255
- gradients: bfloat16 [16384], P(('groups', 'rows')), parts along dimension 0, may hold values from -6 to 6
- hessians: bfloat16 [16384], P(('groups', 'rows')), parts along dimension 0, may hold values from 0.049804688 to 1
- node_ids: int32 [16384], P(('groups', 'rows')), parts along dimension 0, may hold values from 0 to 15
- predictions: float32 [16384], P(('groups', 'rows')), parts along dimension 0, may hold values from -6 to 6
- split_feature: int32 [32], P('groups'), parts along dimension 0, may hold values from 0 to 511
- split_bin: int32 [32], P('groups'), parts along dimension 0, may hold values from 0 to 254
Outputs:
- gains: float32 [1024, 16, 256], P(('groups', 'rows')), parts along dimension 0
- best_gain: float32 [32], P('groups'), parts along dimension 0
- leaf_values: float32 [2, 32], P(None, 'groups'), parts along dimension 1
- new_predictions: float32 [16384], P(('groups', 'rows')), parts along dimension 0
There are 2 independent parts, one for each index of `groups`. A program takes and returns all parts, laid end to end along the dimension named above; each array names one. Nothing has to cross between parts.
All inputs are finite; a program needn't handle non-finite values.
Results may differ from a plain program's by a relative error of at most 0.0003.
Values sent between devices are 32-bit elements; how exact they have to be, the bound alone decides.
A program may use at most 64 MiB of HBM per device.

v0:
```python
import math

import jax
import jax.numpy as jnp
from jax import lax
from jax.sharding import PartitionSpec as P

F = 512
BINS = 256
NODES = 16


l2_penalty = 1.0
shrinkage = 0.5


def combined_all(part, axis, combine):
    gathered = jax.tree.map(lambda a: lax.all_gather(a, axis), part)

    def take(source):
        return jax.tree.map(lambda a: lax.dynamic_index_in_dim(a, source, 0, False), gathered)

    return lax.fori_loop(
        1, lax.axis_size(axis), lambda source, state: combine(state, take(source)), take(0)
    )


def node_weights(node_ids, gradients, hessians):
    node_hot = node_ids[:, None] == jnp.arange(NODES, dtype=jnp.int32)[None, :]
    zero_value = jnp.zeros((), jnp.bfloat16)
    grad_part = jnp.where(node_hot, gradients[:, None], zero_value)
    hess_part = jnp.where(node_hot, hessians[:, None], zero_value)
    return jnp.concatenate([grad_part, hess_part], axis=1)


def bin_onehot(columns):
    return (columns[:, :, None] == jnp.arange(BINS, dtype=jnp.int32)[None, None, :]).astype(
        jnp.bfloat16
    )


def combine_pair(earlier, later):
    return (jnp.maximum(earlier[0], later[0]), earlier[1] + later[1])


def body(bin_ids, gradients, hessians, node_ids, predictions, split_feature, split_bin):
    owned = F // lax.axis_size("rows")
    first_feature = lax.axis_index("rows") * owned
    weights = node_weights(node_ids, gradients, hessians)
    feat_block = math.gcd(F, 32)

    def one_block(block_index):
        columns = lax.dynamic_slice_in_dim(bin_ids, block_index * feat_block, feat_block, 1)
        return jnp.einsum(
            "rk,rfb->fkb", weights, bin_onehot(columns), preferred_element_type=jnp.float32
        )

    blocks = lax.map(one_block, jnp.arange(F // feat_block, dtype=jnp.int32))
    full_terms = blocks.reshape(F, 2 * NODES, BINS)
    histogram = lax.psum_scatter(full_terms, "rows", scatter_dimension=0, tiled=True)
    cum_grad = jnp.cumsum(histogram[:, :NODES], axis=2)
    cum_hess = jnp.cumsum(histogram[:, NODES:], axis=2)
    tot_grad = cum_grad[:, :, -1:]
    tot_hess = cum_hess[:, :, -1:]
    gains = 0.5 * (
        cum_grad**2 / (cum_hess + l2_penalty)
        + (tot_grad - cum_grad) ** 2 / (tot_hess - cum_hess + l2_penalty)
        - tot_grad**2 / (tot_hess + l2_penalty)
    )
    best_local = jnp.max(gains, axis=(0, 2))
    local_feature = split_feature - first_feature
    owner_sel = jnp.arange(owned, dtype=jnp.int32)[:, None] == local_feature[None, :]
    bin_sel = jnp.arange(BINS, dtype=jnp.int32)[None, :] == split_bin[:, None]
    picked = owner_sel[:, :, None] & bin_sel[None, :, :]
    left_grad = jnp.sum(jnp.where(picked, cum_grad, 0.0), axis=(0, 2))
    left_hess = jnp.sum(jnp.where(picked, cum_hess, 0.0), axis=(0, 2))
    node_grad = jnp.sum(jnp.where(owner_sel, tot_grad[:, :, 0], 0.0), axis=0)
    node_hess = jnp.sum(jnp.where(owner_sel, tot_hess[:, :, 0], 0.0), axis=0)
    leaf_local = jnp.stack([left_grad, left_hess, node_grad, node_hess])
    best_gain, leaf_stats = combined_all((best_local, leaf_local), "rows", combine_pair)
    leaf_left = -leaf_stats[0] / (leaf_stats[1] + l2_penalty)
    leaf_right = -(leaf_stats[2] - leaf_stats[0]) / (leaf_stats[3] - leaf_stats[1] + l2_penalty)
    leaf_values = jnp.stack([leaf_left, leaf_right])
    node_hot = node_ids[:, None] == jnp.arange(NODES, dtype=jnp.int32)[None, :]
    row_feature = jnp.sum(jnp.where(node_hot, split_feature[None, :], 0), axis=1)
    row_threshold = jnp.sum(jnp.where(node_hot, split_bin[None, :], 0), axis=1)
    row_bin = jnp.take_along_axis(bin_ids, row_feature[:, None], axis=1)[:, 0]
    left_row = jnp.sum(jnp.where(node_hot, leaf_left[None, :], 0.0), axis=1)
    right_row = jnp.sum(jnp.where(node_hot, leaf_right[None, :], 0.0), axis=1)
    new_predictions = predictions + shrinkage * jnp.where(
        row_bin > row_threshold, right_row, left_row
    )
    return (gains, best_gain, leaf_values, new_predictions)


def solution(mesh):
    return jax.shard_map(
        body,
        mesh=mesh,
        in_specs=(
            P(("groups", "rows"), None),
            P(("groups", "rows")),
            P(("groups", "rows")),
            P(("groups", "rows")),
            P(("groups", "rows")),
            P("groups"),
            P("groups"),
        ),
        out_specs=(
            P(("groups", "rows"), None, None),
            P("groups"),
            P(None, "groups"),
            P(("groups", "rows")),
        ),
        check_vma=False,
    )
```

profile of v0, /device:TPU:0, one launch (start us, length us, event | category | flops | bytes accessed | tf_op | source)
XLA Modules:
  0.0 398.6 jit_solution(5753148695925994905)
XLA Ops:
  7.2 1.6 copy.50
  9.5 107.6 %while.27 = (s32[]{:T(128)}, f32[16,32,32,256]{3,2,1,0:T(8,128)}, s32[16]{0:T(128)S(1)}, s32[512,512]{0,1:T(8,128)S(1)}, bf16[512,32]{0,1:T(8,128)(2,1)S(1)}, /*...) while((s32[]{:T(128)}, f32[16,32,32,256]{3,2,1,0:T(8,128)}, s32[16]{0:T(128)S(1)}, ...), condition=%wide.region_1.2_spmd, body=%wide.region_0.1_spmd.sunk | while | flops 272629760 | bytes 1278619 | solution.py:58
  10.8 5.5 %fusion.21 = f32[16,32,32,256]{3,2,1,0:T(8,128)} fusion(f32[16,32,32,256]{3,2,1,0:T(8,128)} %get-tuple-element.296, s32[]{:T(128)} %get-tuple-element.295, s32[512,32]{0,1:T(8,128)S(1)} %constant_dynamic-slice_fusion.2, bf16[512,32]{0,1:T(8,128)(2,1)S(1)} %get-tuple-element.308), kind=kOutput, calls=%fused_computation.5.clone.1 | convolution fusion | flops 272629760 | bytes 1147392 | tf_op jit(solution)/shard_map/while/body/eval_jaxpr/rk,rfb->fkb/dot_general | solution.py:54
  17.5 5.5 %fusion.21 = f32[16,32,32,256]{3,2,1,0:T(8,128)} fusion(f32[16,32,32,256]{3,2,1,0:T(8,128)} %get-tuple-element.296, s32[]{:T(128)} %get-tuple-element.295, s32[512,32]{0,1:T(8,128)S(1)} %constant_dynamic-slice_fusion.2, bf16[512,32]{0,1:T(8,128)(2,1)S(1)} %get-tuple-element.308), kind=kOutput, calls=%fused_computation.5.clone.1 | convolution fusion | flops 272629760 | bytes 1147392 | tf_op jit(solution)/shard_map/while/body/eval_jaxpr/rk,rfb->fkb/dot_general | solution.py:54
  24.2 5.5 %fusion.21 = f32[16,32,32,256]{3,2,1,0:T(8,128)} fusion(f32[16,32,32,256]{3,2,1,0:T(8,128)} %get-tuple-element.296, s32[]{:T(128)} %get-tuple-element.295, s32[512,32]{0,1:T(8,128)S(1)} %constant_dynamic-slice_fusion.2, bf16[512,32]{0,1:T(8,128)(2,1)S(1)} %get-tuple-element.308), kind=kOutput, calls=%fused_computation.5.clone.1 | convolution fusion | flops 272629760 | bytes 1147392 | tf_op jit(solution)/shard_map/while/body/eval_jaxpr/rk,rfb->fkb/dot_general | solution.py:54
  31.0 5.5 %fusion.21 = f32[16,32,32,256]{3,2,1,0:T(8,128)} fusion(f32[16,32,32,256]{3,2,1,0:T(8,128)} %get-tuple-element.296, s32[]{:T(128)} %get-tuple-element.295, s32[512,32]{0,1:T(8,128)S(1)} %constant_dynamic-slice_fusion.2, bf16[512,32]{0,1:T(8,128)(2,1)S(1)} %get-tuple-element.308), kind=kOutput, calls=%fused_computation.5.clone.1 | convolution fusion | flops 272629760 | bytes 1147392 | tf_op jit(solution)/shard_map/while/body/eval_jaxpr/rk,rfb->fkb/dot_general | solution.py:54
  37.7 5.5 %fusion.21 = f32[16,32,32,256]{3,2,1,0:T(8,128)} fusion(f32[16,32,32,256]{3,2,1,0:T(8,128)} %get-tuple-element.296, s32[]{:T(128)} %get-tuple-element.295, s32[512,32]{0,1:T(8,128)S(1)} %constant_dynamic-slice_fusion.2, bf16[512,32]{0,1:T(8,128)(2,1)S(1)} %get-tuple-element.308), kind=kOutput, calls=%fused_computation.5.clone.1 | convolution fusion | flops 272629760 | bytes 1147392 | tf_op jit(solution)/shard_map/while/body/eval_jaxpr/rk,rfb->fkb/dot_general | solution.py:54
  44.4 5.5 %fusion.21 = f32[16,32,32,256]{3,2,1,0:T(8,128)} fusion(f32[16,32,32,256]{3,2,1,0:T(8,128)} %get-tuple-element.296, s32[]{:T(128)} %get-tuple-element.295, s32[512,32]{0,1:T(8,128)S(1)} %constant_dynamic-slice_fusion.2, bf16[512,32]{0,1:T(8,128)(2,1)S(1)} %get-tuple-element.308), kind=kOutput, calls=%fused_computation.5.clone.1 | convolution fusion | flops 272629760 | bytes 1147392 | tf_op jit(solution)/shard_map/while/body/eval_jaxpr/rk,rfb->fkb/dot_general | solution.py:54
  51.1 5.5 %fusion.21 = f32[16,32,32,256]{3,2,1,0:T(8,128)} fusion(f32[16,32,32,256]{3,2,1,0:T(8,128)} %get-tuple-element.296, s32[]{:T(128)} %get-tuple-element.295, s32[512,32]{0,1:T(8,128)S(1)} %constant_dynamic-slice_fusion.2, bf16[512,32]{0,1:T(8,128)(2,1)S(1)} %get-tuple-element.308), kind=kOutput, calls=%fused_computation.5.clone.1 | convolution fusion | flops 272629760 | bytes 1147392 | tf_op jit(solution)/shard_map/while/body/eval_jaxpr/rk,rfb->fkb/dot_general | solution.py:54
  57.9 5.5 %fusion.21 = f32[16,32,32,256]{3,2,1,0:T(8,128)} fusion(f32[16,32,32,256]{3,2,1,0:T(8,128)} %get-tuple-element.296, s32[]{:T(128)} %get-tuple-element.295, s32[512,32]{0,1:T(8,128)S(1)} %constant_dynamic-slice_fusion.2, bf16[512,32]{0,1:T(8,128)(2,1)S(1)} %get-tuple-element.308), kind=kOutput, calls=%fused_computation.5.clone.1 | convolution fusion | flops 272629760 | bytes 1147392 | tf_op jit(solution)/shard_map/while/body/eval_jaxpr/rk,rfb->fkb/dot_general | solution.py:54
  64.6 5.5 %fusion.21 = f32[16,32,32,256]{3,2,1,0:T(8,128)} fusion(f32[16,32,32,256]{3,2,1,0:T(8,128)} %get-tuple-element.296, s32[]{:T(128)} %get-tuple-element.295, s32[512,32]{0,1:T(8,128)S(1)} %constant_dynamic-slice_fusion.2, bf16[512,32]{0,1:T(8,128)(2,1)S(1)} %get-tuple-element.308), kind=kOutput, calls=%fused_computation.5.clone.1 | convolution fusion | flops 272629760 | bytes 1147392 | tf_op jit(solution)/shard_map/while/body/eval_jaxpr/rk,rfb->fkb/dot_general | solution.py:54
  71.3 5.5 %fusion.21 = f32[16,32,32,256]{3,2,1,0:T(8,128)} fusion(f32[16,32,32,256]{3,2,1,0:T(8,128)} %get-tuple-element.296, s32[]{:T(128)} %get-tuple-element.295, s32[512,32]{0,1:T(8,128)S(1)} %constant_dynamic-slice_fusion.2, bf16[512,32]{0,1:T(8,128)(2,1)S(1)} %get-tuple-element.308), kind=kOutput, calls=%fused_computation.5.clone.1 | convolution fusion | flops 272629760 | bytes 1147392 | tf_op jit(solution)/shard_map/while/body/eval_jaxpr/rk,rfb->fkb/dot_general | solution.py:54
  78.0 5.5 %fusion.21 = f32[16,32,32,256]{3,2,1,0:T(8,128)} fusion(f32[16,32,32,256]{3,2,1,0:T(8,128)} %get-tuple-element.296, s32[]{:T(128)} %get-tuple-element.295, s32[512,32]{0,1:T(8,128)S(1)} %constant_dynamic-slice_fusion.2, bf16[512,32]{0,1:T(8,128)(2,1)S(1)} %get-tuple-element.308), kind=kOutput, calls=%fused_computation.5.clone.1 | convolution fusion | flops 272629760 | bytes 1147392 | tf_op jit(solution)/shard_map/while/body/eval_jaxpr/rk,rfb->fkb/dot_general | solution.py:54
  84.7 5.5 %fusion.21 = f32[16,32,32,256]{3,2,1,0:T(8,128)} fusion(f32[16,32,32,256]{3,2,1,0:T(8,128)} %get-tuple-element.296, s32[]{:T(128)} %get-tuple-element.295, s32[512,32]{0,1:T(8,128)S(1)} %constant_dynamic-slice_fusion.2, bf16[512,32]{0,1:T(8,128)(2,1)S(1)} %get-tuple-element.308), kind=kOutput, calls=%fused_computation.5.clone.1 | convolution fusion | flops 272629760 | bytes 1147392 | tf_op jit(solution)/shard_map/while/body/eval_jaxpr/rk,rfb->fkb/dot_general | solution.py:54
  91.5 5.5 %fusion.21 = f32[16,32,32,256]{3,2,1,0:T(8,128)} fusion(f32[16,32,32,256]{3,2,1,0:T(8,128)} %get-tuple-element.296, s32[]{:T(128)} %get-tuple-element.295, s32[512,32]{0,1:T(8,128)S(1)} %constant_dynamic-slice_fusion.2, bf16[512,32]{0,1:T(8,128)(2,1)S(1)} %get-tuple-element.308), kind=kOutput, calls=%fused_computation.5.clone.1 | convolution fusion | flops 272629760 | bytes 1147392 | tf_op jit(solution)/shard_map/while/body/eval_jaxpr/rk,rfb->fkb/dot_general | solution.py:54
  98.2 5.5 %fusion.21 = f32[16,32,32,256]{3,2,1,0:T(8,128)} fusion(f32[16,32,32,256]{3,2,1,0:T(8,128)} %get-tuple-element.296, s32[]{:T(128)} %get-tuple-element.295, s32[512,32]{0,1:T(8,128)S(1)} %constant_dynamic-slice_fusion.2, bf16[512,32]{0,1:T(8,128)(2,1)S(1)} %get-tuple-element.308), kind=kOutput, calls=%fused_computation.5.clone.1 | convolution fusion | flops 272629760 | bytes 1147392 | tf_op jit(solution)/shard_map/while/body/eval_jaxpr/rk,rfb->fkb/dot_general | solution.py:54
  104.9 5.5 %fusion.21 = f32[16,32,32,256]{3,2,1,0:T(8,128)} fusion(f32[16,32,32,256]{3,2,1,0:T(8,128)} %get-tuple-element.296, s32[]{:T(128)} %get-tuple-element.295, s32[512,32]{0,1:T(8,128)S(1)} %constant_dynamic-slice_fusion.2, bf16[512,32]{0,1:T(8,128)(2,1)S(1)} %get-tuple-element.308), kind=kOutput, calls=%fused_computation.5.clone.1 | convolution fusion | flops 272629760 | bytes 1147392 | tf_op jit(solution)/shard_map/while/body/eval_jaxpr/rk,rfb->fkb/dot_general | solution.py:54
  111.6 5.5 %fusion.21 = f32[16,32,32,256]{3,2,1,0:T(8,128)} fusion(f32[16,32,32,256]{3,2,1,0:T(8,128)} %get-tuple-element.296, s32[]{:T(128)} %get-tuple-element.295, s32[512,32]{0,1:T(8,128)S(1)} %constant_dynamic-slice_fusion.2, bf16[512,32]{0,1:T(8,128)(2,1)S(1)} %get-tuple-element.308), kind=kOutput, calls=%fused_computation.5.clone.1 | convolution fusion | flops 272629760 | bytes 1147392 | tf_op jit(solution)/shard_map/while/body/eval_jaxpr/rk,rfb->fkb/dot_general | solution.py:54
  118.4 4.5 %gather_fusion = s32[512]{0:T(512)S(1)} fusion(s32[512,512]{1,0:T(8,128)S(1)} %copy-done, s32[512]{0:T(512)S(1)} %bitcast.82), kind=kCustom, calls=%fused_computation | custom fusion | bytes 8192 | tf_op jit(solution)/shard_map/jit(take_along_axis)/gather | solution.py:87
  124.2 173.2 %reduce-scatter.2.cloned.1.call-done = f32[32,32,256]{2,1,0:T(8,128)} async-done(((f32[512,32,256]{2,1,0:T(8,128)}), f32[32,32,256]{2,1,0:T(8,128)}) %reduce-scatter.2.cloned.1.call-update) | async-done | bytes 1048592 | tf_op jit(solution)/shard_map/reduce_scatter | solution.py:60
  298.8 18.1 %reduce-window.14 = f32[32,16,2,128]{3,1,2,0:T(8,128)S(1)} reduce-window(f32[32,16,2,128]{3,1,2,0:T(8,128)S(1)} %get-tuple-element.223, f32[]{:T(128)} %constant.92.clone.1), window={size=1x1x1x128 pad=0_0x0_0x0_0x127_0}, to_apply=%region_3.4 | reduce-window | flops 16646144 | bytes 1048580 | tf_op jit(solution)/shard_map/reduce-window
  318.4 18.1 %reduce-window.16 = f32[32,16,2,128]{3,1,2,0:T(8,128)S(1)} reduce-window(f32[32,16,2,128]{3,1,2,0:T(8,128)S(1)} %get-tuple-element.222, f32[]{:T(128)} %constant.92.clone.1), window={size=1x1x1x128 pad=0_0x0_0x0_0x127_0}, to_apply=%region_5.6 | reduce-window | flops 16646144 | bytes 1048580 | tf_op jit(solution)/shard_map/reduce-window.2
  339.5 31.5 %all-reduce = f32[256]{0:T(256)S(1)} all-reduce(f32[256]{0:T(256)S(1)} %dynamic-update-slice), channel_id=2, replica_groups=mesh['groups'=2,'rows'=16] {'rows'}, use_global_device_ids=true, to_apply=%add | all-reduce | flops 256 | bytes 2048
  372.4 17.2 %all-gather.2 = f32[16,4,16]{2,1,0:T(4,128)S(1)} all-gather(f32[1,4,16]{2,1,0:T(4,128)S(1)} %maximum_bitcast_fusion), channel_id=3, replica_groups=mesh['groups'=2,'rows'=16] {'rows'}, dimensions={0}, use_global_device_ids=true | all-gather | bytes 4352 | tf_op jit(solution)/shard_map/all_gather | solution.py:18
  (129 shorter events, 21.9 us)
Async XLA Ops:
  7.2 290.2 %reduce-scatter.2.cloned.1.call-start = ((), (), s32[]{:S(2)}) async-start(), calls=%async_computation.1 | async-start | bytes 17825792 | tf_op jit(solution)/shard_map/reduce_scatter | solution.py:60
  117.1 0.7 copy-start.5
  117.1 0.8 copy-start.1
  117.1 0.8 copy-start.4
  117.1 1.3 copy-start
  117.1 5.8 %copy-start.6 = (u32[32]{0:T(128)S(1)}, u32[32]{0:T(128)}, u32[]{:S(2)}) copy-start(u32[32]{0:T(128)} %constant.118) | copy-start | bytes 388
  117.1 274.0 %copy-start.3 = (f32[512]{0:T(512)S(1)}, f32[512]{0:T(512)}, u32[]{:S(2)}) copy-start(f32[512]{0:T(512)} %param.15) | copy-start | bytes 6148
  390.4 1.3 copy-start.2
Sparse Core Ops, SparseCore 0:
  117.3 180.0 reduce-scatter.1
where the time goes:
time: 399 us
  waiting for transfers between devices  173 us (43%)
  matrix products  87.4 us (22%)
  blocking collectives  48.7 us (12%)
  other arithmetic  42 us (11%)
  local copies, waits for them, and re-layouts  21.3 us (5%)
  between operations  14.9 us (4%)
  loops' own time  11 us (3%)
    reduce_scatter x1, waiting for transfers between devices, body(): lax.psum_scatter(full_terms, 'rows', scatter_dimension=0, tiled=True)  173 us
    dot_general x16, matrix products, one_block(): jnp.einsum('rk,rfb->fkb', weights, bin_onehot(columns), preferred_element...  87.4 us
    another operation x6, other arithmetic  36.8 us
    unnamed x1, blocking collectives  31.5 us
    all_gather x1, blocking collectives, combined_all(): gathered = jax.tree.map(lambda a: lax.all_gather(a, axis), part)  17.2 us
    another operation x1, loops' own time, body(): blocks = lax.map(one_block, jnp.arange(F // feat_block, dtype=jnp.int32))  10.6 us
    dynamic_slice x16, local copies, waits for them, and re-layouts, body(): blocks = lax.map(one_block, jnp.arange(F // feat_block, dtype=jnp.int32))  9.32 us
  transfers between devices with their start and end apart: 1, of which 1 were waited for; matrix products, arithmetic and copies ran while one was open for 1% of the time, Pallas kernels for 0%

commit v1 on v0

v1 whole, which is shorter than its diff:
```python
import functools

import jax
import jax.numpy as jnp
from jax import lax
from jax.experimental import pallas as pl
from jax.experimental.pallas import tpu as pltpu
from jax.sharding import PartitionSpec as P

BINS = 256
NODES = 16
LANES = 128
HALVES = BINS // LANES

l2_penalty = 1.0
shrinkage = 0.5

f32 = jnp.float32
bf16 = jnp.bfloat16


def flipped(me, step, n):
    if n & (n - 1):
        return (step + n - me) % n
    out, bit = 0, 1
    while bit < n:
        out = out + (((me // bit) % 2 + (step // bit) % 2) % 2) * bit
        bit *= 2
    return out


def to_row(column):
    shape = (column.shape[0], LANES)
    diagonal = lax.broadcasted_iota(jnp.int32, shape, 0) == lax.broadcasted_iota(
        jnp.int32, shape, 1
    )
    return jnp.sum(jnp.where(diagonal, column, 0.0), axis=0, keepdims=True)


def kernel(
    n,
    bins_ref,
    rows_ref,
    split_ref,
    gains_ref,
    best_ref,
    leaf_ref,
    pred_ref,
    send_bins,
    send_meta,
    recv_bins,
    recv_meta,
    send_best,
    recv_best,
    acc,
    bins_out,
    bins_in,
    meta_out,
    meta_in,
    best_out,
    best_in,
):
    owned = recv_bins.shape[1]
    local = recv_bins.shape[2]
    features = owned * n
    me = lax.axis_index("rows")

    barrier = pltpu.get_barrier_semaphore()

    def greet(step, carry):
        pl.semaphore_signal(
            barrier, inc=1, device_id={"rows": flipped(me, step, n)},
            device_id_type=pl.DeviceIdType.MESH,
        )
        return carry

    def all_steps(body):
        lax.fori_loop(1, n, body, 0)

    all_steps(greet)

    width = min(features, LANES)
    chosen = split_ref[:, 0:1]
    node_bin = jnp.zeros((NODES, local), f32)
    for tile in range(features // width):
        turned = jnp.transpose(bins_ref[:, tile * width : (tile + 1) * width].astype(f32))
        for j in range(width // owned):
            send_bins[tile * (width // owned) + j] = turned[j * owned : (j + 1) * owned]
        feature = lax.broadcasted_iota(jnp.int32, (NODES, width), 1) + tile * width
        pick = jnp.where(feature == chosen, 1.0, 0.0).astype(bf16)
        node_bin = node_bin + jnp.dot(
            pick, turned.astype(bf16), preferred_element_type=f32
        )

    node = lax.broadcasted_iota(jnp.int32, (NODES, local), 0).astype(f32)
    node_hot = node == rows_ref[2:3]
    beyond = node_bin > split_ref[:, 1:2].astype(f32)
    side = jnp.sum(jnp.where(node_hot & beyond, 1.0, 0.0), axis=0, keepdims=True)
    send_meta[0:3] = rows_ref[0:3]
    send_meta[3:4] = side
    recv_bins[me] = send_bins[me]
    recv_meta[me] = send_meta[...]

    pl.semaphore_wait(barrier, n - 1)

    def bins_copy(step):
        to = flipped(me, step, n)
        return pltpu.make_async_remote_copy(
            src_ref=send_bins.at[to], dst_ref=recv_bins.at[me],
            send_sem=bins_out.at[to], recv_sem=bins_in.at[me],
            device_id={"rows": to}, device_id_type=pl.DeviceIdType.MESH,
        )

    def meta_copy(step):
        to = flipped(me, step, n)
        return pltpu.make_async_remote_copy(
            src_ref=send_meta, dst_ref=recv_meta.at[me],
            send_sem=meta_out.at[to], recv_sem=meta_in.at[me],
            device_id={"rows": to}, device_id_type=pl.DeviceIdType.MESH,
        )

    def best_copy(step):
        to = flipped(me, step, n)
        return pltpu.make_async_remote_copy(
            src_ref=send_best, dst_ref=recv_best.at[me],
            send_sem=best_out.at[to], recv_sem=best_in.at[me],
            device_id={"rows": to}, device_id_type=pl.DeviceIdType.MESH,
        )

    def landed(buffer, sems, source):
        pltpu.make_async_copy(buffer.at[source], buffer.at[source], sems.at[source]).wait()

    def start(step, carry):
        meta_copy(step).start()
        bins_copy(step).start()
        return carry

    all_steps(start)

    acc[...] = jnp.zeros_like(acc)
    low = lax.broadcasted_iota(jnp.int32, (LANES, LANES), 0).astype(bf16)
    low = jnp.concatenate([low] * (local // LANES), axis=1)
    one = jnp.ones((), bf16)
    zero = jnp.zeros((), bf16)
    group = 4 if owned % 4 == 0 else 1

    def accumulate(step, sums):
        left_sum, node_sum = sums
        source = flipped(me, step, n)

        @pl.when(step > 0)
        def _():
            landed(recv_meta, meta_in, source)
            landed(recv_bins, bins_in, source)

        meta = recv_meta[source]
        hot = node == meta[2:3]
        exact = jnp.concatenate(
            [jnp.where(hot, meta[0:1], 0.0), jnp.where(hot, meta[1:2], 0.0)], axis=0
        )
        left = jnp.where(meta[3:4] == 0.0, exact, 0.0)
        for tile in range(local // LANES):
            lanes = slice(tile * LANES, (tile + 1) * LANES)
            left_sum = left_sum + left[:, lanes]
            node_sum = node_sum + exact[:, lanes]
        weights = exact.astype(bf16)

        def some_features(block, carry):
            for j in range(group):
                f = block * group + j
                row = recv_bins[source, pl.ds(f, 1), :]
                high = jnp.floor(row * (1.0 / LANES))
                rest = (row - high * LANES).astype(bf16)
                high = jnp.broadcast_to(high.astype(bf16), weights.shape)
                upto = jnp.where(rest <= low, one, zero)
                parts = [weights] + [
                    jnp.where(high == float(h), weights, zero) for h in range(1, HALVES)
                ]
                acc[f] += lax.dot_general(
                    jnp.concatenate(parts, axis=0), upto, (((1,), (1,)), ((), ())),
                    preferred_element_type=f32,
                )
            return carry

        lax.fori_loop(0, owned // group, some_features, 0)
        return left_sum, node_sum

    blank = jnp.zeros((2 * NODES, LANES), f32)
    left_sum, node_sum = lax.fori_loop(0, n, accumulate, (blank, blank))

    def score(f, best):
        table = acc[f]
        upper = [table[2 * NODES * h : 2 * NODES * (h + 1)] for h in range(1, HALVES)]
        first = table[0 : 2 * NODES]
        for part in upper:
            first = first - part
        offset = jnp.zeros((2 * NODES, 1), f32)
        sums = []
        for part in [first] + upper:
            sums.append(part + offset)
            offset = offset + part[:, LANES - 1 : LANES]
        tot_grad, tot_hess = offset[:NODES], offset[NODES:]
        whole = tot_grad * tot_grad / (tot_hess + l2_penalty)
        for h, part in enumerate(sums):
            cum_grad, cum_hess = part[:NODES], part[NODES:]
            rest_grad = tot_grad - cum_grad
            gain = 0.5 * (
                cum_grad * cum_grad / (cum_hess + l2_penalty)
                + rest_grad * rest_grad / (tot_hess - cum_hess + l2_penalty)
                - whole
            )
            gains_ref[f, :, h * LANES : (h + 1) * LANES] = gain
            best = jnp.maximum(best, gain)
        return best

    best = lax.fori_loop(0, owned, score, jnp.full((NODES, LANES), -jnp.inf, f32))
    send_best[...] = to_row(jnp.max(best, axis=1, keepdims=True))
    recv_best[me] = send_best[...]

    def start_best(step, carry):
        best_copy(step).start()
        return carry

    all_steps(start_best)

    left_sum = jnp.sum(left_sum, axis=1, keepdims=True)
    node_sum = jnp.sum(node_sum, axis=1, keepdims=True)
    left_grad, left_hess = left_sum[:NODES], left_sum[NODES:]
    right_grad = node_sum[:NODES] - left_grad
    right_hess = node_sum[NODES:] - left_hess
    leaf_left = -left_grad / (left_hess + l2_penalty)
    leaf_right = -right_grad / (right_hess + l2_penalty)
    leaf_ref[0:1] = to_row(leaf_left)
    leaf_ref[1:2] = to_row(leaf_right)
    value = jnp.where(beyond, leaf_right, leaf_left)
    moved = jnp.sum(jnp.where(node_hot, value, 0.0), axis=0, keepdims=True)
    pred_ref[...] = rows_ref[3:4] + shrinkage * moved

    def finish(step, carry):
        meta_copy(step).wait_send()
        bins_copy(step).wait_send()
        best_copy(step).wait_send()
        landed(recv_best, best_in, flipped(me, step, n))
        return carry

    all_steps(finish)
    best_ref[...] = jnp.max(recv_best[...], axis=0)


def body(n, bin_ids, gradients, hessians, node_ids, predictions, split_feature, split_bin):
    local, features = bin_ids.shape
    owned = features // n
    rows = jnp.stack(
        [gradients.astype(f32), hessians.astype(f32), node_ids.astype(f32), predictions]
    )
    splits = jnp.stack([split_feature, split_bin], axis=1)
    vmem = pl.BlockSpec(memory_space=pltpu.VMEM)
    gains, best, leaf, pred = pl.pallas_call(
        functools.partial(kernel, n),
        out_shape=(
            jax.ShapeDtypeStruct((owned, NODES, BINS), f32),
            jax.ShapeDtypeStruct((1, LANES), f32),
            jax.ShapeDtypeStruct((2, LANES), f32),
            jax.ShapeDtypeStruct((1, local), f32),
        ),
        in_specs=[vmem] * 3,
        out_specs=(vmem,) * 4,
        scratch_shapes=[
            pltpu.VMEM((n, owned, local), f32),
            pltpu.VMEM((4, local), f32),
            pltpu.VMEM((n, owned, local), f32),
            pltpu.VMEM((n, 4, local), f32),
            pltpu.VMEM((1, LANES), f32),
            pltpu.VMEM((n, 1, LANES), f32),
            pltpu.VMEM((owned, 2 * NODES * HALVES, LANES), f32),
        ]
        + [pltpu.SemaphoreType.DMA((n,))] * 6,
        compiler_params=pltpu.CompilerParams(
            collective_id=0, has_side_effects=True, vmem_limit_bytes=48 << 20
        ),
        name="split_finding",
    )(bin_ids, rows, splits)
    return gains, best[0, :NODES], leaf[:, :NODES], pred[0]


def solution(mesh):
    both = P(("groups", "rows"))
    return jax.shard_map(
        functools.partial(body, mesh.shape["rows"]),
        mesh=mesh,
        in_specs=(
            P(("groups", "rows"), None), both, both, both, both, P("groups"), P("groups"),
        ),
        out_specs=(P(("groups", "rows"), None, None), P("groups"), P(None, "groups"), both),
        check_vma=False,
    )
```

time: 399 us -> 62.7 us (0.16)
  waiting for transfers between devices: 173 us -> 0 us
  matrix products: 87.4 us -> 0 us
  Pallas kernels: 0 us -> 54.6 us
  blocking collectives: 48.7 us -> 0 us
  other arithmetic: 42 us -> 0.03 us
  between operations: 14.9 us -> 0.67 us
  local copies, waits for them, and re-layouts: 21.3 us -> 7.11 us
  loops' own time: 11 us -> 0 us
    reduce_scatter x1 -> x0, waiting for transfers between devices: 173 us -> none  [body(): lax.psum_scatter(full_terms, 'rows', scatter_dimension=0, tiled=True)]
    dot_general x16 -> x0, matrix products: 87.4 us -> none  [one_block(): jnp.einsum('rk,rfb->fkb', weights, bin_onehot(columns), preferred_element...]
    pallas_call x0 -> x1, Pallas kernels: none -> 54.6 us  [body(): pl.pallas_call(functools.partial(kernel, n), out_shape=(jax.ShapeDtypeStr...]
    another operation x7 -> x4, other arithmetic: 37.4 us -> 0.03 us  [the longest x3 0.02 us: body(): jnp.stack([gradients.astype(f32), hessians.astype(f32), node_ids.astype(f...]
    unnamed x1 -> x0, blocking collectives: 31.5 us -> none
    all_gather x1 -> x0, blocking collectives: 17.2 us -> none  [combined_all(): gathered = jax.tree.map(lambda a: lax.all_gather(a, axis), part)]
    another operation x2 -> x0, loops' own time: 11 us -> none  [the longest x1 10.6 us: body(): blocks = lax.map(one_block, jnp.arange(F // feat_block, dtype=jnp.int32))]
    dynamic_slice x34 -> x0, local copies, waits for them, and re-layouts: 9.51 us -> none  [the longest x16 9.32 us: body(): blocks = lax.map(one_block, jnp.arange(F // feat_block, dtype=jnp.int32))]
  transfers between devices with their start and end apart: 1 -> 0, of which waited for: 1 -> 0; matrix products, arithmetic and copies ran while one was open for 1% -> 0% of each run, Pallas kernels for 0% -> 0%
where the time goes in v1:
time: 62.7 us; the launch traced here: 62.4 us
  Pallas kernels  54.6 us (87%)
  local copies, waits for them, and re-layouts  7.11 us (11%)
  between operations  0.67 us (1%)
    pallas_call x1, Pallas kernels, body(): pl.pallas_call(functools.partial(kernel, n), out_shape=(jax.ShapeDtypeStr...  54.6 us
    unnamed x17, local copies, waits for them, and re-layouts  6.52 us

profile of v1, /device:TPU:0, one launch (start us, length us, event | category | flops | bytes accessed | tf_op | source)
XLA Modules:
  0.0 62.4 jit_solution(9120448747192370436)
XLA Ops:
  0.6 0.0 copy-start.5
  0.6 0.0 copy-start.6
  0.7 0.6 %copy-done.5 = s32[16]{0:T(128)S(1)} copy-done((s32[16]{0:T(128)S(1)}, s32[16]{0:T(128)}, u32[]{:S(2)}) %copy-start.5) | copy-done | bytes 88
  1.3 0.0 copy-done.6
  1.3 0.0 copy-start.3
  1.3 0.7 %copy-done.3 = bf16[512]{0:T(512)(128)(2,1)S(1)} copy-done((bf16[512]{0:T(512)(128)(2,1)S(1)}, bf16[512]{0:T(512)(128)(2,1)}, u32[]{:S(2)}) %copy-start.3) | copy-done | bytes 1048
  2.0 0.0 copy-start.4
  2.0 0.7 %copy-done.4 = bf16[512]{0:T(512)(128)(2,1)S(1)} copy-done((bf16[512]{0:T(512)(128)(2,1)S(1)}, bf16[512]{0:T(512)(128)(2,1)}, u32[]{:S(2)}) %copy-start.4) | copy-done | bytes 1048
  2.7 0.0 copy-start.1
  2.7 0.7 %copy-done.1 = s32[512]{0:T(512)S(1)} copy-done((s32[512]{0:T(512)S(1)}, s32[512]{0:T(512)}, u32[]{:S(2)}) %copy-start.1) | copy-done | bytes 2072
  3.3 0.0 copy-start.2
  3.4 0.7 %copy-done.2 = f32[512]{0:T(512)S(1)} copy-done((f32[512]{0:T(512)S(1)}, f32[512]{0:T(512)}, u32[]{:S(2)}) %copy-start.2) | copy-done | bytes 2072
  4.0 0.1 copy.13.split_ref
  4.1 0.0 copy-start
  4.1 1.2 %copy-done = s32[512,512]{1,0:T(8,128)S(1)} copy-done((s32[512,512]{1,0:T(8,128)S(1)}, s32[512,512]{1,0:T(8,128)}, u32[]{:S(2)}) %copy-start) | copy-done | bytes 1048600
  5.4 54.6 %split_finding.1 = (f32[32,16,256]{2,1,0:T(8,128)S(1)}, f32[1,128]{1,0:T(1,128)S(1)}, f32[2,128]{1,0:T(2,128)S(1)}, f32[1,512]{1,0:T(1,128)S(1)}) custom-call(s32[512,512]{1,0:T(8,128)S(1)} %copy-done, f32[4,512]{1,0:T(4,128)S(1)} %pad_maximum_fusion.rows_ref, s32[16,2]{1,0:T(8,128)S(1)} %copy.13.split_ref), custom_call_target="tpu_custom_call" | custom-call | tf_op jit(solution)/shard_map/split_finding/pallas_call | solution.py:258
  60.0 0.5 slice_bitcast_fusion
  60.5 0.8 %copy.17 = f32[32,16,256]{2,1,0:T(8,128)} copy(f32[32,16,256]{2,1,0:T(8,128)S(1)} %get-tuple-element.16) | data formatting | bytes 1048576
  61.3 0.6 copy.18
  61.9 0.6 copy.19
  (5 shorter events, 0.0 us)
Async XLA Ops:
  0.6 0.7 %copy-start.5 = (s32[16]{0:T(128)S(1)}, s32[16]{0:T(128)}, u32[]{:S(2)}) copy-start(s32[16]{0:T(128)} %param.13) | copy-start | bytes 196
  0.6 0.7 %copy-start.6 = (s32[16]{0:T(128)S(1)}, s32[16]{0:T(128)}, u32[]{:S(2)}) copy-start(s32[16]{0:T(128)} %param.12) | copy-start | bytes 196
  1.3 0.7 %copy-start.3 = (bf16[512]{0:T(512)(128)(2,1)S(1)}, bf16[512]{0:T(512)(128)(2,1)}, u32[]{:S(2)}) copy-start(bf16[512]{0:T(512)(128)(2,1)} %param.8) | copy-start | bytes 3076
  2.0 0.7 %copy-start.4 = (bf16[512]{0:T(512)(128)(2,1)S(1)}, bf16[512]{0:T(512)(128)(2,1)}, u32[]{:S(2)}) copy-start(bf16[512]{0:T(512)(128)(2,1)} %param.9) | copy-start | bytes 3076
  2.7 0.7 %copy-start.1 = (s32[512]{0:T(512)S(1)}, s32[512]{0:T(512)}, u32[]{:S(2)}) copy-start(s32[512]{0:T(512)} %param.10) | copy-start | bytes 6148
  3.3 0.7 %copy-start.2 = (f32[512]{0:T(512)S(1)}, f32[512]{0:T(512)}, u32[]{:S(2)}) copy-start(f32[512]{0:T(512)} %param.11) | copy-start | bytes 6148
  4.1 1.2 %copy-start = (s32[512,512]{1,0:T(8,128)S(1)}, s32[512,512]{1,0:T(8,128)}, u32[]{:S(2)}) copy-start(s32[512,512]{1,0:T(8,128)} %bins_ref.1) | copy-start | bytes 3145732

commit v2 on v1

v2 whole, which is shorter than its diff:
```python
import functools
import math

import jax
import jax.numpy as jnp
from jax import lax
from jax.experimental import pallas as pl
from jax.experimental.pallas import tpu as pltpu
from jax.sharding import PartitionSpec as P

BINS = 256
NODES = 16
LANES = 128
HALVES = BINS // LANES

l2_penalty = 1.0
shrinkage = 0.5

f32 = jnp.float32
bf16 = jnp.bfloat16


def flipped(me, step, n):
    out, bit = 0, 1
    while bit < n:
        out = out + (((me // bit) % 2 + (step // bit) % 2) % 2) * bit
        bit *= 2
    return out


def to_row(column):
    shape = (column.shape[0], LANES)
    diagonal = lax.broadcasted_iota(jnp.int32, shape, 0) == lax.broadcasted_iota(
        jnp.int32, shape, 1
    )
    return jnp.sum(jnp.where(diagonal, column, 0.0), axis=0, keepdims=True)


def to_column(row):
    shape = (row.shape[1], row.shape[1])
    diagonal = lax.broadcasted_iota(jnp.int32, shape, 0) == lax.broadcasted_iota(
        jnp.int32, shape, 1
    )
    return jnp.sum(jnp.where(diagonal, row, 0.0), axis=1, keepdims=True)


def in_one_row(packed):
    pieces = [packed[j : j + 1].astype(f32) for j in range(packed.shape[0])]
    return jnp.concatenate(pieces, axis=1)


def kernel(
    n,
    bins_hbm,
    grad_hbm,
    hess_hbm,
    node_hbm,
    pred_hbm,
    feature_hbm,
    bin_hbm,
    gains_ref,
    best_ref,
    leaf_ref,
    pred_ref,
    bins_ref,
    grad_ref,
    hess_ref,
    node_ref,
    old_ref,
    feature_ref,
    bin_ref,
    send_bins,
    send_meta,
    recv_bins,
    recv_meta,
    send_stat,
    recv_stat,
    send_best,
    recv_best,
    acc,
    tile_sem,
    small_sem,
    bins_out,
    bins_in,
    meta_out,
    meta_in,
    stat_out,
    stat_in,
    best_out,
    best_in,
):
    owned = recv_bins.shape[1]
    local = recv_bins.shape[2]
    features = owned * n
    me = lax.axis_index("rows")
    width = bins_ref.shape[2]
    tiles = features // width
    per_tile = width // owned

    small = [
        pltpu.make_async_copy(source, target, small_sem.at[i])
        for i, (source, target) in enumerate(
            [
                (grad_hbm, grad_ref),
                (hess_hbm, hess_ref),
                (node_hbm, node_ref),
                (feature_hbm, feature_ref),
                (bin_hbm, bin_ref),
                (pred_hbm, old_ref),
            ]
        )
    ]
    for copy in small:
        copy.start()

    order = list(range(tiles))
    mine = me // per_tile
    tile_at = [flipped(mine, s, tiles) for s in order]
    loads = []
    for i, tile in enumerate(tile_at):
        columns = pl.ds(pl.multiple_of(tile * width, width), width)
        loads.append(
            pltpu.make_async_copy(bins_hbm.at[:, columns], bins_ref.at[i], tile_sem.at[i])
        )
        loads[-1].start()

    barrier = pltpu.get_barrier_semaphore()

    def all_steps(body):
        lax.fori_loop(1, n, body, 0)

    def greet(step, carry):
        pl.semaphore_signal(
            barrier, inc=1, device_id={"rows": flipped(me, step, n)},
            device_id_type=pl.DeviceIdType.MESH,
        )
        return carry

    all_steps(greet)

    def remote(to, source, target, out_sem, in_sem):
        return pltpu.make_async_remote_copy(
            src_ref=source, dst_ref=target.at[me],
            send_sem=out_sem.at[to], recv_sem=in_sem.at[me],
            device_id={"rows": to}, device_id_type=pl.DeviceIdType.MESH,
        )

    def bins_copy(to):
        return remote(to, send_bins.at[to], recv_bins, bins_out, bins_in)

    def meta_copy(to):
        return remote(to, send_meta, recv_meta, meta_out, meta_in)

    def stat_copy(to):
        return remote(to, send_stat, recv_stat, stat_out, stat_in)

    def best_copy(to):
        return remote(to, send_best, recv_best, best_out, best_in)

    def landed(buffer, sems, source):
        pltpu.make_async_copy(buffer.at[source], buffer.at[source], sems.at[source]).wait()

    for copy in small:
        copy.wait()
    send_meta[0:1] = in_one_row(grad_ref[...])
    send_meta[1:2] = in_one_row(hess_ref[...])
    send_meta[2:3] = node_ref[...].astype(f32)
    recv_meta[me] = send_meta[...]
    chosen = to_column(feature_ref[...].astype(f32))
    threshold = to_column(bin_ref[...].astype(f32))
    node = lax.broadcasted_iota(jnp.int32, (NODES, local), 0).astype(f32)
    node_hot = node == send_meta[2:3]

    pl.semaphore_wait(barrier, n - 1)

    def start_meta(step, carry):
        meta_copy(flipped(me, step, n)).start()
        return carry

    def send_tile(tile):
        def start(j, carry):
            to = tile * per_tile + flipped(me % per_tile, j, per_tile)

            @pl.when(to != me)
            def _():
                bins_copy(to).start()

            return carry

        lax.fori_loop(0, per_tile, start, 0)

    node_bin = jnp.zeros((NODES, local), f32)
    for i, tile in enumerate(tile_at):
        loads[i].wait()
        turned = jnp.transpose(bins_ref[i].astype(f32))
        for j in range(per_tile):
            send_bins[tile * per_tile + j] = turned[j * owned : (j + 1) * owned]
        if i == 0:
            all_steps(start_meta)
        else:
            send_tile(tile_at[i - 1])
        feature = lax.broadcasted_iota(jnp.int32, (NODES, width), 1) + tile * width
        pick = jnp.where(feature.astype(f32) == chosen, 1.0, 0.0).astype(bf16)
        node_bin = node_bin + jnp.dot(
            pick, turned.astype(bf16), preferred_element_type=f32
        )
    send_tile(tile_at[-1])
    recv_bins[me] = send_bins[me]

    beyond = node_bin > threshold
    for i, hot in enumerate((node_hot & jnp.logical_not(beyond), node_hot)):
        exact = jnp.concatenate(
            [jnp.where(hot, send_meta[0:1], 0.0), jnp.where(hot, send_meta[1:2], 0.0)], axis=0
        )
        send_stat[i : i + 1] = to_row(jnp.sum(exact, axis=1, keepdims=True))
    recv_stat[me] = send_stat[...]

    acc[...] = jnp.zeros_like(acc)
    low = lax.broadcasted_iota(jnp.int32, (LANES, LANES), 0).astype(bf16)
    low = jnp.concatenate([low] * (local // LANES), axis=1)
    one = jnp.ones((), bf16)
    zero = jnp.zeros((), bf16)
    group = math.gcd(owned, 32)

    def accumulate(step, carry):
        source = flipped(me, step, n)

        @pl.when(step > 0)
        def _():
            landed(recv_meta, meta_in, source)
            landed(recv_bins, bins_in, source)

        @pl.when(step == 1)
        def _():
            all_steps(start_stat)

        meta = recv_meta[source]
        hot = node == meta[2:3]
        weights = jnp.concatenate(
            [jnp.where(hot, meta[0:1], 0.0), jnp.where(hot, meta[1:2], 0.0)], axis=0
        ).astype(bf16)

        def some_features(block, carry):
            at = pl.ds(pl.multiple_of(block * group, group), group)
            row = recv_bins[source, at, :]
            highs = jnp.floor(row * (1.0 / LANES))
            rests = row - highs * LANES
            sums = []
            for j in range(group):
                rest = jnp.broadcast_to(rests[j : j + 1], (LANES, local)).astype(bf16)
                high = jnp.broadcast_to(highs[j : j + 1], weights.shape).astype(bf16)
                upto = jnp.where(rest <= low, one, zero)
                parts = [weights] + [
                    jnp.where(high == float(h), weights, zero) for h in range(1, HALVES)
                ]
                sums.append(
                    lax.dot_general(
                        jnp.concatenate(parts, axis=0), upto, (((1,), (1,)), ((), ())),
                        preferred_element_type=f32,
                    )
                )
            block_acc = acc.at[at]
            for j in range(group):
                block_acc[j] += sums[j]
            return carry

        return lax.fori_loop(0, owned // group, some_features, carry)

    def start_stat(step, carry):
        stat_copy(flipped(me, step, n)).start()
        return carry

    lax.fori_loop(0, n, accumulate, 0)

    def score(f, best):
        table = acc[f]
        upper = [table[2 * NODES * h : 2 * NODES * (h + 1)] for h in range(1, HALVES)]
        first = table[0 : 2 * NODES]
        for part in upper:
            first = first - part
        offset = jnp.zeros((2 * NODES, 1), f32)
        sums = []
        for part in [first] + upper:
            sums.append(part + offset)
            offset = offset + part[:, LANES - 1 : LANES]
        tot_grad, tot_hess = offset[:NODES], offset[NODES:]
        whole = tot_grad * tot_grad / (tot_hess + l2_penalty)
        for h, part in enumerate(sums):
            cum_grad, cum_hess = part[:NODES], part[NODES:]
            rest_grad = tot_grad - cum_grad
            gain = 0.5 * (
                cum_grad * cum_grad / (cum_hess + l2_penalty)
                + rest_grad * rest_grad / (tot_hess - cum_hess + l2_penalty)
                - whole
            )
            gains_ref[f, :, h * LANES : (h + 1) * LANES] = gain
            best = jnp.maximum(best, gain)
        return best

    best = lax.fori_loop(0, owned, score, jnp.full((NODES, LANES), -jnp.inf, f32))
    send_best[...] = to_row(jnp.max(best, axis=1, keepdims=True))
    recv_best[me] = send_best[...]

    def start_best(step, carry):
        best_copy(flipped(me, step, n)).start()
        return carry

    all_steps(start_best)

    def wait_stat(step, carry):
        landed(recv_stat, stat_in, flipped(me, step, n))
        return carry

    all_steps(wait_stat)
    stats = jnp.sum(recv_stat[...], axis=0)
    left_grad, left_hess = stats[0:1, :NODES], stats[0:1, NODES : 2 * NODES]
    node_grad, node_hess = stats[1:2, :NODES], stats[1:2, NODES : 2 * NODES]
    leaf_left = -left_grad / (left_hess + l2_penalty)
    leaf_right = -(node_grad - left_grad) / (node_hess - left_hess + l2_penalty)
    leaf_ref[0:1] = leaf_left
    leaf_ref[1:2] = leaf_right
    value = jnp.where(beyond, to_column(leaf_right), to_column(leaf_left))
    moved = jnp.sum(jnp.where(node_hot, value, 0.0), axis=0, keepdims=True)
    pred_ref[...] = old_ref[...] + shrinkage * moved

    def finish(step, carry):
        partner = flipped(me, step, n)
        meta_copy(partner).wait_send()
        bins_copy(partner).wait_send()
        stat_copy(partner).wait_send()
        best_copy(partner).wait_send()
        landed(recv_best, best_in, partner)
        return carry

    all_steps(finish)
    best_ref[...] = jnp.max(recv_best[...], axis=0)[:, :NODES]


def emit(gains_ref, best_ref, leaf_ref, pred_ref, gains_out, best_out, leaf_out, pred_out, sem):
    copy = pltpu.make_async_copy(gains_ref, gains_out, sem)
    copy.start()
    best_out[...] = best_ref[...]
    leaf_out[...] = leaf_ref[...]
    pred_out[...] = pred_ref[...]
    copy.wait()


def body(n, bin_ids, gradients, hessians, node_ids, predictions, split_feature, split_bin):
    assert n & (n - 1) == 0
    local, features = bin_ids.shape
    owned = features // n
    width = min(features, LANES)
    vmem = pl.BlockSpec(memory_space=pltpu.VMEM)
    hbm = pl.BlockSpec(memory_space=pltpu.HBM)
    shapes = (
        jax.ShapeDtypeStruct((owned, NODES, BINS), f32),
        jax.ShapeDtypeStruct((1, NODES), f32),
        jax.ShapeDtypeStruct((2, NODES), f32),
        jax.ShapeDtypeStruct((1, local), f32),
    )
    packed = (local // LANES, LANES)
    results = pl.pallas_call(
        functools.partial(kernel, n),
        out_shape=shapes,
        in_specs=[hbm] * 7,
        out_specs=(vmem,) * 4,
        scratch_shapes=[
            pltpu.VMEM((features // width, local, width), jnp.int32),
            pltpu.VMEM(packed, bf16),
            pltpu.VMEM(packed, bf16),
            pltpu.VMEM((1, local), jnp.int32),
            pltpu.VMEM((1, local), f32),
            pltpu.VMEM((1, NODES), jnp.int32),
            pltpu.VMEM((1, NODES), jnp.int32),
            pltpu.VMEM((n, owned, local), f32),
            pltpu.VMEM((3, local), f32),
            pltpu.VMEM((n, owned, local), f32),
            pltpu.VMEM((n, 3, local), f32),
            pltpu.VMEM((2, LANES), f32),
            pltpu.VMEM((n, 2, LANES), f32),
            pltpu.VMEM((1, LANES), f32),
            pltpu.VMEM((n, 1, LANES), f32),
            pltpu.VMEM((owned, 2 * NODES * HALVES, LANES), f32),
            pltpu.SemaphoreType.DMA((features // width,)),
            pltpu.SemaphoreType.DMA((6,)),
        ]
        + [pltpu.SemaphoreType.DMA((n,))] * 8,
        compiler_params=pltpu.CompilerParams(
            collective_id=0, has_side_effects=True, vmem_limit_bytes=48 << 20
        ),
        name="split_finding",
    )(
        bin_ids,
        gradients.reshape(packed),
        hessians.reshape(packed),
        node_ids.reshape(1, local),
        predictions.reshape(1, local),
        split_feature.reshape(1, NODES),
        split_bin.reshape(1, NODES),
    )
    gains, best, leaf, pred = pl.pallas_call(
        emit,
        out_shape=shapes,
        in_specs=[vmem] * 4,
        out_specs=(hbm, pl.BlockSpec(), pl.BlockSpec(), pl.BlockSpec()),
        scratch_shapes=[pltpu.SemaphoreType.DMA],
        name="emit",
    )(*results)
    return gains, best[0], leaf, pred[0]


def solution(mesh):
    both = P(("groups", "rows"))
    return jax.shard_map(
        functools.partial(body, mesh.shape["rows"]),
        mesh=mesh,
        in_specs=(
            P(("groups", "rows"), None), both, both, both, both, P("groups"), P("groups"),
        ),
        out_specs=(P(("groups", "rows"), None, None), P("groups"), P(None, "groups"), both),
        check_vma=False,
    )
```

time: 62.7 us -> 53.1 us (0.85)
  Pallas kernels: 54.6 us -> 48.4 us
  local copies, waits for them, and re-layouts: 7.11 us -> 3.78 us
    pallas_call x1 -> x2, Pallas kernels: 54.6 us -> 48.4 us  [the longest x1 45.9 us: body(): pl.pallas_call(functools.partial(kernel, n), out_shape=shapes, in_specs=[...]
    unnamed x17 -> x22, local copies, waits for them, and re-layouts: 6.52 us -> 3.78 us
where the time goes in v2:
time: 53.1 us; the launch traced here: 52.9 us
  Pallas kernels  48.4 us (91%)
  local copies, waits for them, and re-layouts  3.78 us (7%)
  between operations  0.7 us (1%)
    pallas_call x1, Pallas kernels, body(): pl.pallas_call(functools.partial(kernel, n), out_shape=shapes, in_specs=[...  45.9 us
    unnamed x22, local copies, waits for them, and re-layouts  3.78 us
    pallas_call x1, Pallas kernels, body(): pl.pallas_call(emit, out_shape=shapes, in_specs=[vmem] * 4, out_specs=(hb...  2.43 us

profile of v2, /device:TPU:0, one launch (start us, length us, event | category | flops | bytes accessed | tf_op | source)
XLA Modules:
  0.0 52.9 jit_solution(10456597322346670269)
XLA Ops:
  0.6 0.0 copy-start.6
  0.6 0.0 copy-start.9
  0.7 0.0 copy-start.3
  0.7 0.0 copy-start.2
  0.7 0.0 copy-start.5
  0.7 0.0 copy-start.8
  0.7 0.6 %copy-done.6 = bf16[512]{0:T(512)(128)(2,1)S(1)} copy-done((bf16[512]{0:T(512)(128)(2,1)S(1)}, bf16[512]{0:T(512)(128)(2,1)}, u32[]{:S(2)}) %copy-start.6) | copy-done | bytes 1048
  1.3 0.0 copy-done.9
  1.3 0.0 copy-done.3
  1.3 0.0 copy-done.2
  1.4 0.0 copy-done.5
  1.4 0.0 copy-done.8
  1.4 0.0 copy-start
  1.4 1.2 %copy-done = s32[512,512]{1,0:T(8,128)S(1)} copy-done((s32[512,512]{1,0:T(8,128)S(1)}, s32[512,512]{1,0:T(8,128)}, u32[]{:S(2)}) %copy-start) | copy-done | bytes 1048600
  2.6 45.9 %split_finding.1 = (f32[32,16,256]{2,1,0:T(8,128)S(1)}, f32[1,16]{1,0:T(1,128)S(1)}, f32[2,16]{1,0:T(2,128)S(1)}, f32[1,512]{1,0:T(1,128)S(1)}) custom-call(s32[512,512]{1,0:T(8,128)S(1)} %copy-done, bf16[4,128]{1,0:T(4,128)(2,1)S(1)} %bitcast.10, bf16[4,128]{1,0:T(4,128)(2,1)S(1)} %bitcast.11, s32[1,512]{1,0:T(1,128)S(1)} %bitcast.8, f32[1,512]{1,0:T(1,128)S(1)} %bitcast.9, ...), custom_call_target="tpu_custom_call" | custom-call | tf_op jit(solution)/shard_map/split_finding/pallas_call | solution.py:362
  48.6 0.0 copy-start.1
  48.6 0.8 %copy-done.1 = f32[32,16,256]{2,1,0:T(8,128)} copy-done((f32[32,16,256]{2,1,0:T(8,128)}, f32[32,16,256]{2,1,0:T(8,128)S(1)}, u32[]{:S(2)}) %copy-start.1) | copy-done | bytes 524312
  49.4 0.0 copy-start.10
  49.4 0.5 copy-done.10
  49.8 0.0 copy-start.7
  49.9 0.0 copy-start.4
  49.9 0.6 %copy-done.7 = f32[2,16]{1,0:T(2,128)} copy-done((f32[2,16]{1,0:T(2,128)}, f32[2,16]{1,0:T(2,128)S(1)}, u32[]{:S(2)}) %copy-start.7) | copy-done | bytes 152
  50.4 0.0 copy-done.4
  50.4 2.4 %emit.1 = (f32[32,16,256]{2,1,0:T(8,128)}, f32[1,16]{1,0:T(1,128)}, f32[2,16]{1,0:T(2,128)}, f32[1,512]{1,0:T(1,128)}) custom-call(f32[32,16,256]{2,1,0:T(8,128)} %copy-done.1, f32[1,16]{1,0:T(1,128)} %copy-done.10, f32[2,16]{1,0:T(2,128)} %copy-done.7, f32[1,512]{1,0:T(1,128)} %copy-done.4), custom_call_target="tpu_custom_call" | custom-call | tf_op jit(solution)/shard_map/emit/pallas_call | solution.py:401
Async XLA Ops:
  0.6 0.7 %copy-start.6 = (bf16[512]{0:T(512)(128)(2,1)S(1)}, bf16[512]{0:T(512)(128)(2,1)}, u32[]{:S(2)}) copy-start(bf16[512]{0:T(512)(128)(2,1)} %param.9) | copy-start | bytes 3076
  0.6 0.7 %copy-start.9 = (s32[16]{0:T(128)S(1)}, s32[16]{0:T(128)}, u32[]{:S(2)}) copy-start(s32[16]{0:T(128)} %param.13) | copy-start | bytes 196
  0.7 0.7 %copy-start.3 = (f32[512]{0:T(512)S(1)}, f32[512]{0:T(512)}, u32[]{:S(2)}) copy-start(f32[512]{0:T(512)} %param.11) | copy-start | bytes 6148
  0.7 0.7 %copy-start.2 = (s32[512]{0:T(512)S(1)}, s32[512]{0:T(512)}, u32[]{:S(2)}) copy-start(s32[512]{0:T(512)} %param.10) | copy-start | bytes 6148
  0.7 0.7 %copy-start.5 = (bf16[512]{0:T(512)(128)(2,1)S(1)}, bf16[512]{0:T(512)(128)(2,1)}, u32[]{:S(2)}) copy-start(bf16[512]{0:T(512)(128)(2,1)} %param.8) | copy-start | bytes 3076
  0.7 0.7 %copy-start.8 = (s32[16]{0:T(128)S(1)}, s32[16]{0:T(128)}, u32[]{:S(2)}) copy-start(s32[16]{0:T(128)} %param.12) | copy-start | bytes 196
  1.4 1.2 %copy-start = (s32[512,512]{1,0:T(8,128)S(1)}, s32[512,512]{1,0:T(8,128)}, u32[]{:S(2)}) copy-start(s32[512,512]{1,0:T(8,128)} %bins_hbm.1) | copy-start | bytes 3145732
  48.6 0.8 %copy-start.1 = (f32[32,16,256]{2,1,0:T(8,128)}, f32[32,16,256]{2,1,0:T(8,128)S(1)}, u32[]{:S(2)}) copy-start(f32[32,16,256]{2,1,0:T(8,128)S(1)} %get-tuple-element.12.gains_ref) | copy-start | bytes 1572868
  49.4 0.5 copy-start.10
  49.8 0.6 %copy-start.7 = (f32[2,16]{1,0:T(2,128)}, f32[2,16]{1,0:T(2,128)S(1)}, u32[]{:S(2)}) copy-start(f32[2,16]{1,0:T(2,128)S(1)} %get-tuple-element.14.leaf_ref) | copy-start | bytes 388
  49.9 0.6 %copy-start.4 = (f32[1,512]{1,0:T(1,128)}, f32[1,512]{1,0:T(1,128)S(1)}, u32[]{:S(2)}) copy-start(f32[1,512]{1,0:T(1,128)S(1)} %get-tuple-element.15.pred_ref) | copy-start | bytes 6148

commit v3 on v2

--- a/solution.py
+++ b/solution.py
@@ -336,15 +336,6 @@
     best_ref[...] = jnp.max(recv_best[...], axis=0)[:, :NODES]
 
 
-def emit(gains_ref, best_ref, leaf_ref, pred_ref, gains_out, best_out, leaf_out, pred_out, sem):
-    copy = pltpu.make_async_copy(gains_ref, gains_out, sem)
-    copy.start()
-    best_out[...] = best_ref[...]
-    leaf_out[...] = leaf_ref[...]
-    pred_out[...] = pred_ref[...]
-    copy.wait()
-
-
 def body(n, bin_ids, gradients, hessians, node_ids, predictions, split_feature, split_bin):
     assert n & (n - 1) == 0
     local, features = bin_ids.shape
@@ -386,7 +377,7 @@
         ]
         + [pltpu.SemaphoreType.DMA((n,))] * 8,
         compiler_params=pltpu.CompilerParams(
-            collective_id=0, has_side_effects=True, vmem_limit_bytes=48 << 20
+            collective_id=0, has_side_effects=True, vmem_limit_bytes=60 * 1024 * 1024
         ),
         name="split_finding",
     )(
@@ -398,14 +389,7 @@
         split_feature.reshape(1, NODES),
         split_bin.reshape(1, NODES),
     )
-    gains, best, leaf, pred = pl.pallas_call(
-        emit,
-        out_shape=shapes,
-        in_specs=[vmem] * 4,
-        out_specs=(hbm, pl.BlockSpec(), pl.BlockSpec(), pl.BlockSpec()),
-        scratch_shapes=[pltpu.SemaphoreType.DMA],
-        name="emit",
-    )(*results)
+    gains, best, leaf, pred = results
     return gains, best[0], leaf, pred[0]
 
 

time: 53.1 us -> 51 us (0.960)
  Pallas kernels: 48.4 us -> 46.7 us
    pallas_call x1 -> x0, Pallas kernels: 2.43 us -> none  [body(): pl.pallas_call(emit, out_shape=shapes, in_specs=[vmem] * 4, out_specs=(hb...]
    pallas_call x1, Pallas kernels: 45.9 us -> 46.7 us  [body(): pl.pallas_call(functools.partial(kernel, n), out_shape=shapes, in_specs=[...]
    unnamed x22 -> x10, local copies, waits for them, and re-layouts: 3.78 us -> 3.53 us
where the time goes in v3:
time: 51 us; the launch traced here: 50.8 us
  Pallas kernels  46.7 us (92%)
  local copies, waits for them, and re-layouts  3.53 us (7%)
  between operations  0.66 us (1%)
    pallas_call x1, Pallas kernels, body(): pl.pallas_call(functools.partial(kernel, n), out_shape=shapes, in_specs=[...  46.7 us
    unnamed x10, local copies, waits for them, and re-layouts  3.53 us

profile of v3, /device:TPU:0, one launch (start us, length us, event | category | flops | bytes accessed | tf_op | source)
XLA Modules:
  0.0 50.8 jit_solution(7599971722216166825)
XLA Ops:
  0.6 46.7 %split_finding.1 = (f32[32,16,256]{2,1,0:T(8,128)}, f32[1,16]{1,0:T(1,128)}, f32[2,16]{1,0:T(2,128)}, f32[1,512]{1,0:T(1,128)}) custom-call(s32[512,512]{1,0:T(8,128)} %bins_hbm.1, bf16[4,128]{1,0:T(4,128)(2,1)} %bitcast.11, bf16[4,128]{1,0:T(4,128)(2,1)} %bitcast.12, s32[1,512]{1,0:T(1,128)} %bitcast.8, f32[1,512]{1,0:T(1,128)} %bitcast.9, ...), custom_call_target="tpu_custom_call" | custom-call | tf_op jit(solution)/shard_map/split_finding/pallas_call | solution.py:353
  47.3 0.0 copy-start.2
  47.3 0.0 copy-start.1
  47.3 1.9 %copy.15 = f32[32,16,256]{2,1,0:T(8,128)} copy(f32[32,16,256]{2,1,0:T(8,128)} %get-tuple-element.16) | data formatting | bytes 1048576
  49.2 0.0 copy-done.2
  49.2 0.0 copy-start
  49.2 0.5 %copy.16 = f32[16]{0:T(128)} copy(f32[16]{0:T(128)S(1)} %bitcast.15) | data formatting | bytes 128
  49.7 0.0 copy-done.1
  49.7 0.6 %copy.17 = f32[2,16]{1,0:T(2,128)} copy(f32[2,16]{1,0:T(2,128)S(1)} %copy-done.1) | data formatting | bytes 256
  50.3 0.0 copy-done
  50.3 0.6 %copy.18 = f32[512]{0:T(512)} copy(f32[512]{0:T(512)S(1)} %bitcast.10) | data formatting | bytes 4096
Async XLA Ops:
  47.3 1.9 %copy-start.2 = (f32[1,16]{1,0:T(1,128)S(1)}, f32[1,16]{1,0:T(1,128)}, u32[]{:S(2)}) copy-start(f32[1,16]{1,0:T(1,128)} %get-tuple-element.9) | copy-start | bytes 196
  47.3 2.4 %copy-start.1 = (f32[2,16]{1,0:T(2,128)S(1)}, f32[2,16]{1,0:T(2,128)}, u32[]{:S(2)}) copy-start(f32[2,16]{1,0:T(2,128)} %get-tuple-element.18) | copy-start | bytes 388
  49.2 1.1 %copy-start = (f32[1,512]{1,0:T(1,128)S(1)}, f32[1,512]{1,0:T(1,128)}, u32[]{:S(2)}) copy-start(f32[1,512]{1,0:T(1,128)} %get-tuple-element.11) | copy-start | bytes 6148
